TPU v7x, 512 devices: a whole 4x4x16 slice. The times are simulated.
512 devices in a mesh: ia: 64 (over x, z_lo, core), jb: 8 (over y, z_hi).
Axes of the slice: x: 4, y: 4, z: 16 (z_hi: 2, z_lo: 8; z = z_hi * 8 + z_lo), core: 2. Of those that a mesh axis runs over, the one named last changes fastest.
Arguments:
- density: bfloat16 [8000, 100000], P('ia', 'jb'), may hold values from -6 to 6
- chol_vectors: bfloat16 [100000, 512], P('jb', 'ia'), may hold values from -0.01953125 to 0.01953125
- virt_coef: bfloat16 [1000, 1100], P('jb'), may hold values from -0.1875 to 0.1875
Outputs:
- half_back: float32 [8, 512, 1100], P(None, ('ia', 'jb'))
All inputs are finite; a program needn't handle non-finite values.
Results may differ from a plain program's by a relative error of at most 0.0003.
Values may be sent and summed in bfloat16 or wider, within the bound.
No kernel may reach another device: no remote copies, remote signals or barrier semaphores. Data moves between devices by JAX's collectives and lax.ppermute only.
A program may use at most 64 MiB of HBM per device.

v0:
```python
import jax
import jax.numpy as jnp
from jax import lax
from jax.sharding import Mesh
from jax.sharding import PartitionSpec as P

JB = ("jb_0", "jb_1")
IA_JB = ("ia", "jb_0", "jb_1")


def from_root(shard, axis, root):
    return lax.dynamic_index_in_dim(lax.all_gather(shard, axis), root, 0, keepdims=False)


def summed_rows(shard, axes, dim):
    for axis in axes:
        shard = lax.psum_scatter(shard, axis, scatter_dimension=dim, tiled=True)
    return shard


def on_device(density, chol_vectors, virt_coef):
    row_count = density.shape[0]
    groups = lax.axis_size(JB)
    slab_devices = lax.axis_size("ia")
    all_vectors = lax.all_gather(chol_vectors, "ia", axis=1, tiled=True)
    gamma_part = jnp.dot(density, all_vectors, preferred_element_type=jnp.float32)
    owner_row = lax.axis_index("ia") % groups
    coef_block = from_root(virt_coef, JB, owner_row).astype(jnp.float32)
    chol_count = gamma_part.shape[1]
    group_width = chol_count // slab_devices
    reduced = summed_rows(gamma_part.reshape(row_count, slab_devices, group_width), JB, 2)
    summed = jnp.einsum("arq,an->rqn", reduced, coef_block, precision=lax.Precision.HIGHEST)
    regrouped = lax.all_to_all(summed, "ia", split_axis=0, concat_axis=0, tiled=True)
    occ_slab = slab_devices // groups
    return jnp.sum(
        regrouped.reshape(occ_slab, groups, regrouped.shape[1], regrouped.shape[2]), axis=1
    )


def solution(mesh):
    split = Mesh(mesh.devices.reshape(mesh.shape["ia"], 4, 2), ("ia", "jb_0", "jb_1"))
    return jax.shard_map(
        on_device,
        mesh=split,
        in_specs=(P("ia", JB), P(JB, "ia"), P(JB, None)),
        out_specs=P(None, IA_JB, None),
        check_vma=False,
    )
```

profile of v0, /device:TPU:1, one launch (start us, length us, event | category | flops | bytes accessed | tf_op | source)
XLA Modules:
  0.0 315.7 jit_solution(6847420634601952481)
XLA Ops:
  7.4 0.0 copy-start
  7.4 0.0 all-gather.5.cloned.1.call-start
  7.4 0.7 all-gather.5.cloned.1.call-update
  8.1 0.0 reduce-scatter.3.cloned.1.call-start
  8.1 140.4 %all-gather.5.cloned.1.call-done = bf16[12500,512]{0,1:T(8,128)(2,1)} async-done(((bf16[12500,8]{0,1:T(8,128)(2,1)}), bf16[12500,512]{0,1:T(8,128)(2,1)}) %all-gather.5.cloned.1.call-update) | async-done | bytes 12800016 | tf_op jit(solution)/shard_map/all_gather | solution.py:25
  148.5 0.0 copy-done
  148.5 6.5 %convolution_bitcast_fusion.1 = f32[125,64,8]{0,2,1:T(8,128)S(1)} fusion(bf16[125,12500]{0,1:T(8,128)(2,1)S(1)} %copy-done, bf16[12500,512]{0,1:T(8,128)(2,1)} %all-gather.5.cloned.1.call-done), kind=kOutput, calls=%fused_computation.1 | convolution fusion | flops 1600000000 | bytes 16181000 | tf_op jit(solution)/shard_map/dot_general | solution.py:26
  155.1 0.8 copy.6
  155.8 0.0 reduce-scatter.3.cloned.1.call-update
  155.8 0.0 all-gather.7.cloned.1.call-start
  155.9 0.5 all-gather.7.cloned.1.call-update
  156.4 0.0 reduce-scatter.5.cloned.1.call-start
  156.5 21.4 %reduce-scatter.3.cloned.1.call-done = f32[125,64,2]{0,1,2:T(8,128)} async-done(((f32[125,64,8]{0,1,2:T(8,128)}), f32[125,64,2]{0,1,2:T(8,128)}) %reduce-scatter.3.cloned.1.call-update) | async-done | bytes 64016 | tf_op jit(solution)/shard_map/reduce_scatter | solution.py:17
  177.9 0.0 reduce-scatter.5.cloned.1.call-update
  178.0 98.3 %all-gather.7.cloned.1.call-done = bf16[8,125,1100]{1,2,0:T(8,128)(2,1)} async-done(((bf16[1,125,1100]{1,2,0:T(8,128)(2,1)}), bf16[8,125,1100]{1,2,0:T(8,128)(2,1)}) %all-gather.7.cloned.1.call-update) | async-done | bytes 2200016 | tf_op jit(solution)/shard_map/all_gather | solution.py:12
  276.3 0.0 reduce-scatter.5.cloned.1.call-done
  276.3 1.4 convolution_bitcast_fusion
  277.7 0.3 copy.7
  278.0 29.9 %all_to_all.5 = f32[64,1,1100]{2,1,0:T(1,128)S(1)} all-to-all(f32[64,1,1100]{2,1,0:T(1,128)S(1)} %copy.7), channel_id=1, replica_groups=mesh['ia'=64,'jb_0'=4,'jb_1'=2] {'ia'}, dimensions={0} | all-to-all | bytes 563200 | tf_op jit(solution)/shard_map/all_to_all | solution.py:33
  307.9 0.1 bitcast_reduce_fusion
  308.0 0.6 reduce_sum.12
Async XLA Ops:
  7.4 141.2 %copy-start = (bf16[125,12500]{0,1:T(8,128)(2,1)S(1)}, bf16[125,12500]{0,1:T(8,128)(2,1)}, u32[]{:S(2)}) copy-start(bf16[125,12500]{0,1:T(8,128)(2,1)} %param.3) | copy-start | bytes 9375004
  7.4 141.2 %all-gather.5.cloned.1.call-start = ((), (), s32[]{:S(2)}) async-start(), calls=%async_computation.3 | async-start | bytes 13045760 | tf_op jit(solution)/shard_map/all_gather | solution.py:25
  8.1 169.8 %reduce-scatter.3.cloned.1.call-start = ((), (), s32[]{:S(2)}) async-start(), calls=%async_computation.4 | async-start | bytes 327680 | tf_op jit(solution)/shard_map/reduce_scatter | solution.py:17
  155.8 120.4 %all-gather.7.cloned.1.call-start = ((), (), s32[]{:S(2)}) async-start(), calls=%async_computation.6 | async-start | bytes 2543616 | tf_op jit(solution)/shard_map/all_gather | solution.py:12
  156.4 119.9 %reduce-scatter.5.cloned.1.call-start = ((), (), s32[]{:S(2)}) async-start(), calls=%async_computation.5 | async-start | bytes 98304 | tf_op jit(solution)/shard_map/reduce_scatter | solution.py:17
Sparse Core Ops, SparseCore 0:
  10.3 138.1 all-gather.4
  156.0 21.9 reduce-scatter.2
  180.7 33.1 reduce-scatter.4
Sparse Core Ops, SparseCore 1:
  159.5 116.7 all-gather.6
where the time goes:
time: 316 us
  waiting for transfers between devices  261 us (83%)
  blocking collectives  29.9 us (9%)
  between operations  14.6 us (5%)
  matrix products  7.89 us (2%)
    all_gather x1, waiting for transfers between devices, on_device(): all_vectors = lax.all_gather(chol_vectors, 'ia', axis=1, tiled=True)  140 us
    all_gather x1, waiting for transfers between devices, from_root(): lax.all_gather(shard, axis)  98.3 us
    all_to_all x1, blocking collectives, on_device(): lax.all_to_all(summed, 'ia', split_axis=0, concat_axis=0, tiled=True)  29.9 us
    reduce_scatter x2, waiting for transfers between devices, summed_rows(): shard = lax.psum_scatter(shard, axis, scatter_dimension=dim, tiled=True)  21.4 us
    dot_general x1, matrix products, on_device(): jnp.dot(density, all_vectors, preferred_element_type=jnp.float32)  6.51 us
  transfers between devices with their start and end apart: 4, of which 3 were waited for; matrix products, arithmetic and copies ran while one was open for 0% of the time, Pallas kernels for 0%

commit v1 on v0

--- a/solution.py
+++ b/solution.py
@@ -22,7 +22,15 @@
     row_count = density.shape[0]
     groups = lax.axis_size(JB)
     slab_devices = lax.axis_size("ia")
-    all_vectors = lax.all_gather(chol_vectors, "ia", axis=1, tiled=True)
+    all_vectors = jnp.concatenate(
+        lax.all_to_all(
+            jnp.stack(lax.axis_size("ia") * [chol_vectors], 0),
+            axis_name="ia",
+            concat_axis=0,
+            split_axis=0,
+        ),
+        1,
+    )
     gamma_part = jnp.dot(density, all_vectors, preferred_element_type=jnp.float32)
     owner_row = lax.axis_index("ia") % groups
     coef_block = from_root(virt_coef, JB, owner_row).astype(jnp.float32)

time: 316 us -> 759 us (2.40)
  blocking collectives: 29.9 us -> 605 us
  waiting for transfers between devices: 261 us -> 120 us
    all_to_all x0 -> x1, blocking collectives: none -> 575 us  [on_device(): lax.all_to_all(jnp.stack(lax.axis_size('ia') * [chol_vectors], 0), axis_n...]
    all_gather x1 -> x0, waiting for transfers between devices: 140 us -> none  [on_device(): all_vectors = lax.all_gather(chol_vectors, 'ia', axis=1, tiled=True)]
  transfers between devices with their start and end apart: 4 -> 3, of which waited for: 3 -> 2; matrix products, arithmetic and copies ran while one was open for 0% -> 0% of each run, Pallas kernels for 0% -> 0%
where the time goes in v1:
time: 759 us
  blocking collectives  605 us (80%)
  waiting for transfers between devices  120 us (16%)
  between operations  14.9 us (2%)
  matrix products  10.3 us (1%)
    all_to_all x1, blocking collectives, on_device(): lax.all_to_all(jnp.stack(lax.axis_size('ia') * [chol_vectors], 0), axis_n...  575 us
    all_gather x1, waiting for transfers between devices, from_root(): lax.all_gather(shard, axis)  98.3 us
    all_to_all x1, blocking collectives, on_device(): lax.all_to_all(summed, 'ia', split_axis=0, concat_axis=0, tiled=True)  29.9 us
    reduce_scatter x2, waiting for transfers between devices, summed_rows(): shard = lax.psum_scatter(shard, axis, scatter_dimension=dim, tiled=True)  21.5 us
  transfers between devices with their start and end apart: 3, of which 2 were waited for; matrix products, arithmetic and copies ran while one was open for 0% of the time, Pallas kernels for 0%

profile of v1, /device:TPU:1, one launch (start us, length us, event | category | flops | bytes accessed | tf_op | source)
XLA Modules:
  0.0 758.5 jit_solution(12419605949534010153)
XLA Ops:
  7.4 0.0 copy-start
  7.4 0.0 reduce-scatter.3.cloned.1.call-start
  7.4 6.5 stack.2
  13.9 575.4 %all_to_all.10 = bf16[64,12500,8]{1,2,0:T(8,128)(2,1)} all-to-all(bf16[64,12500,8]{1,2,0:T(8,128)(2,1)} %stack.2), channel_id=1, replica_groups=mesh['ia'=64,'jb_0'=4,'jb_1'=2] {'ia'}, dimensions={0} | all-to-all | bytes 25600000 | tf_op jit(solution)/shard_map/all_to_all | solution.py:26
  589.3 0.0 copy-done
  589.3 8.9 %fusion = f32[125,64,8]{0,1,2:T(8,128)} fusion(bf16[64,8,12500]{2,1,0:T(8,128)(2,1)} %bitcast.21, bf16[125,12500]{0,1:T(8,128)(2,1)S(1)} %copy-done), kind=kOutput, calls=%fused_computation | convolution fusion | flops 1600000000 | bytes 16181000 | tf_op jit(solution)/shard_map/dot_general | solution.py:34
  598.2 0.0 reduce-scatter.3.cloned.1.call-update
  598.2 0.0 all-gather.4.cloned.1.call-start
  598.3 0.5 all-gather.4.cloned.1.call-update
  598.8 0.0 reduce-scatter.5.cloned.1.call-start
  598.9 21.5 %reduce-scatter.3.cloned.1.call-done = f32[125,64,2]{0,1,2:T(8,128)} async-done(((f32[125,64,8]{0,1,2:T(8,128)}), f32[125,64,2]{0,1,2:T(8,128)}) %reduce-scatter.3.cloned.1.call-update) | async-done | bytes 64016 | tf_op jit(solution)/shard_map/reduce_scatter | solution.py:17
  620.4 0.0 reduce-scatter.5.cloned.1.call-update
  620.4 98.3 %all-gather.4.cloned.1.call-done = bf16[8,125,1100]{1,2,0:T(8,128)(2,1)} async-done(((bf16[1,125,1100]{1,2,0:T(8,128)(2,1)}), bf16[8,125,1100]{1,2,0:T(8,128)(2,1)}) %all-gather.4.cloned.1.call-update) | async-done | bytes 2200016 | tf_op jit(solution)/shard_map/all_gather | solution.py:12
  718.8 0.0 reduce-scatter.5.cloned.1.call-done
  718.8 1.4 convolution_bitcast_fusion
  720.2 0.3 copy.7
  720.5 29.9 %all_to_all.11 = f32[64,1,1100]{2,1,0:T(1,128)S(1)} all-to-all(f32[64,1,1100]{2,1,0:T(1,128)S(1)} %copy.7), channel_id=1, replica_groups=mesh['ia'=64,'jb_0'=4,'jb_1'=2] {'ia'}, dimensions={0} | all-to-all | bytes 563200 | tf_op jit(solution)/shard_map/all_to_all | solution.py:41
  750.4 0.1 bitcast_reduce_fusion
  750.4 0.6 reduce_sum.12
Async XLA Ops:
  7.4 581.9 %copy-start = (bf16[125,12500]{0,1:T(8,128)(2,1)S(1)}, bf16[125,12500]{0,1:T(8,128)(2,1)}, u32[]{:S(2)}) copy-start(bf16[125,12500]{0,1:T(8,128)(2,1)} %param.3) | copy-start | bytes 9375004
  7.4 613.0 %reduce-scatter.3.cloned.1.call-start = ((), (), s32[]{:S(2)}) async-start(), calls=%async_computation.4 | async-start | bytes 327680 | tf_op jit(solution)/shard_map/reduce_scatter | solution.py:17
  598.2 120.5 %all-gather.4.cloned.1.call-start = ((), (), s32[]{:S(2)}) async-start(), calls=%async_computation.6 | async-start | bytes 2543616 | tf_op jit(solution)/shard_map/all_gather | solution.py:12
  598.8 120.0 %reduce-scatter.5.cloned.1.call-start = ((), (), s32[]{:S(2)}) async-start(), calls=%async_computation.5 | async-start | bytes 98304 | tf_op jit(solution)/shard_map/reduce_scatter | solution.py:17
Sparse Core Ops, SparseCore 0:
  598.4 21.9 reduce-scatter.2
  623.1 33.1 reduce-scatter.4
Sparse Core Ops, SparseCore 1:
  601.9 116.8 all-gather.3
